TPU v7x, 512 devices: a whole 4x8x8 slice. The times are simulated.
512 devices in a mesh: chan: 16 (over z, x_lo), tm: 32 (over y, x_hi, core).
Axes of the slice: x: 4 (x_hi: 2, x_lo: 2; x = x_hi * 2 + x_lo), y: 8, z: 8, core: 2. Of those that a mesh axis runs over, the one named last changes fastest.
Arguments:
- strain_rate: float32 [4096, 16384], P('chan', 'tm'), may hold values from -64 to 64
Outputs:
- stacks: float32 [128, 8, 13056], P('chan', None, 'tm')
All inputs are finite; a program needn't handle non-finite values.
Results may differ from a plain program's by a relative error of at most 0.0041.
Values may be sent and summed in bfloat16 or wider, within the bound.
A program may use at most 64 MiB of HBM per device.

v0:
```python
import math

import jax
import jax.numpy as jnp
from jax import lax
from jax.sharding import PartitionSpec as P

SRC = 8
MAXLAG = 25
W2 = 64
LAGS = 51


def with_halo(shard, sides, width):
    for axis, dim in sides:
        count, length = (lax.axis_size(axis), shard.shape[dim])
        up = [(i, (i + 1) % count) for i in range(count - 1)]
        down = [(j, i) for i, j in up]
        last = lax.slice_in_dim(shard, length - width, length, axis=dim)
        first = lax.slice_in_dim(shard, 0, width, axis=dim)
        before = lax.ppermute(last, axis, up)
        after = lax.ppermute(first, axis, down)
        shard = jnp.concatenate([before, shard, after], axis=dim)
    return shard


def passed_along(block, axis, distance):
    devices = range(lax.axis_size(axis))
    route = [((i - distance) % len(devices), i) for i in devices]
    return lax.ppermute(block, axis, route)


def running_level(strain_rate):
    padded = with_halo(strain_rate, (("tm", 1),), W2)
    magnitude = jnp.abs(padded)
    window_sums = lax.reduce_window(
        magnitude, jnp.zeros((), jnp.float32), lax.add, (1, 2 * W2 + 1), (1, 1), "VALID"
    )
    return window_sums / (2 * W2 + 1) + 1e-05


def lag_rows(rows, shard_len):
    padded = jnp.pad(rows, ((0, 0), (MAXLAG, MAXLAG)))
    return jnp.stack(
        [
            padded[:, 2 * MAXLAG - position : 2 * MAXLAG - position + shard_len]
            for position in range(LAGS)
        ],
        axis=1,
    )


def correlate(lagged, receivers, stack_scale):
    product = jnp.einsum("slu,bu->sbl", lagged, receivers, preferred_element_type=jnp.float32)
    return (product * stack_scale).reshape(SRC, receivers.shape[0] * LAGS)


def visit_blocks(channel_block, work):
    reach_steps = lax.axis_size("chan") // 4
    results = {}
    current = channel_block
    for position in range(reach_steps):
        current = passed_along(current, "chan", 1)
        results[-(position + 1)] = work(current)
    current = channel_block
    for position in range(reach_steps):
        current = passed_along(current, "chan", -1)
        results[position + 1] = work(current)
    ordered = [results[offset] for offset in sorted(results)]
    return jnp.stack(ordered, axis=1)


def body(strain_rate):
    shard_len = strain_rate.shape[1]
    block_width = strain_rate.shape[0]
    shards = lax.axis_size("tm")
    stack_scale = 1.0 / math.sqrt(shard_len * shards)
    normed = (strain_rate / running_level(strain_rate)).astype(jnp.bfloat16)
    source_rows = normed[:: block_width // SRC]
    lagged = lag_rows(source_rows, shard_len)

    def stack_time(receivers):
        return lax.psum_scatter(
            correlate(lagged, receivers, stack_scale), "tm", scatter_dimension=1, tiled=True
        )

    stacks = visit_blocks(normed, stack_time)
    return stacks


def solution(mesh):
    placed = (P("chan", "tm"),)
    return jax.shard_map(
        body, mesh=mesh, in_specs=placed, out_specs=P("chan", None, "tm"), check_vma=False
    )
```

profile of v0, /device:TPU:1, one launch (start us, length us, event | category | flops | bytes accessed | tf_op | source)
XLA Modules:
  0.0 407.8 jit_solution(18261783069063330482)
XLA Ops:
  7.7 6.0 %collective-permute-start = (f32[256,64]{1,0:T(8,128)S(1)}, f32[256,64]{1,0:T(8,128)S(1)}, u32[]{:S(2)}, u32[]{:S(2)}) collective-permute-start(f32[256,64]{1,0:T(8,128)S(1)} %get-tuple-element.13), channel_id=1, source_target_pairs={{0,1},{1,2},{2,3},{3,4},{4,5},{5,6},{6,7},{7,8},{8,9},{9,10},{10,1... | collective-permute-start | bytes 196616 | tf_op jit(solution)/shard_map/ppermute | solution.py:21
  13.7 4.0 collective-permute-start.1
  17.8 3.7 collective-permute-done.1
  22.0 17.7 %reduce_window.7 = f32[256,512]{0,1:T(8,128)S(1)} reduce-window(f32[256,640]{0,1:T(8,128)S(1)} %copy.1946, f32[]{:T(128)} %constant.2.clone.1), window={size=1x129}, to_apply=%region_0.0 | reduce-window | flops 16777216 | bytes 1179652 | tf_op jit(solution)/shard_map/reduce_window | solution.py:36
  40.1 10.7 %collective-permute-start.6 = (bf16[256,512]{1,0:T(8,128)(2,1)S(1)}, bf16[256,512]{1,0:T(8,128)(2,1)S(1)}, u32[]{:S(2)}, u32[]{:S(2)}) collective-permute-start(bf16[256,512]{1,0:T(8,128)(2,1)S(1)} %divide_convert_fusion), channel_id=1, source_target_pairs={{32,0},{64,32},{96,64},{128,96},{160,128},{192,160},{224,192},{256... | collective-permute-start | bytes 786440 | tf_op jit(solution)/shard_map/ppermute | solution.py:30
  50.8 1.9 collective-permute-start.2
  54.2 1.4 stack.234
  55.6 8.2 %collective-permute-start.7 = (bf16[256,512]{1,0:T(8,128)(2,1)S(1)}, bf16[256,512]{1,0:T(8,128)(2,1)S(1)}, u32[]{:S(2)}, u32[]{:S(2)}) collective-permute-start(bf16[256,512]{1,0:T(8,128)(2,1)S(1)} %collective-permute-done.6), channel_id=1, source_target_pairs={{32,0},{64,32},{96,64},{128,96},{160,128},{192,160},{224,192},{256... | collective-permute-start | bytes 786440 | tf_op jit(solution)/shard_map/ppermute | solution.py:30
  63.7 1.9 collective-permute-start.3
  66.4 1.3 reshape.27
  68.3 1.3 reshape.28
  69.6 8.9 %collective-permute-start.8 = (bf16[256,512]{1,0:T(8,128)(2,1)S(1)}, bf16[256,512]{1,0:T(8,128)(2,1)S(1)}, u32[]{:S(2)}, u32[]{:S(2)}) collective-permute-start(bf16[256,512]{1,0:T(8,128)(2,1)S(1)} %collective-permute-done.7), channel_id=1, source_target_pairs={{32,0},{64,32},{96,64},{128,96},{160,128},{192,160},{224,192},{256... | collective-permute-start | bytes 786440 | tf_op jit(solution)/shard_map/ppermute | solution.py:30
  78.8 1.9 collective-permute-start.4
  81.4 1.3 reshape.26
  83.1 1.3 reshape.29
  84.3 8.0 %collective-permute-start.9 = (bf16[256,512]{1,0:T(8,128)(2,1)S(1)}, bf16[256,512]{1,0:T(8,128)(2,1)}, u32[]{:S(2)}, u32[]{:S(2)}) collective-permute-start(bf16[256,512]{1,0:T(8,128)(2,1)S(1)} %collective-permute-done.8), channel_id=1, source_target_pairs={{32,0},{64,32},{96,64},{128,96},{160,128},{192,160},{224,192},{256... | collective-permute-start | bytes 786440 | tf_op jit(solution)/shard_map/ppermute | solution.py:30
  92.7 1.9 collective-permute-start.5
  95.3 1.3 reshape.30
  97.0 1.3 reshape.25
  98.3 1.3 fusion
  99.9 1.3 reshape.31
  102.6 1.3 reshape.24
  103.9 1.3 dynamic-slice
  105.9 288.0 %all-reduce.12.cloned.1.call-done = (f32[8,13056]{1,0:T(8,128)}, f32[8,13056]{1,0:T(8,128)}, f32[8,13056]{1,0:T(8,128)}, f32[8,13056]{1,0:T(8,128)}, f32[8,13056...) async-done(((f32[8,13056]{1,0:T(8,128)}, f32[8,13056]{1,0:T(8,128)}, f32[8,13056]{1,0:T(8,128)}, f32[8,13056]{1,0:T(8,128)}, ...) | async-done | bytes 3342352
  (97 shorter events, 15.9 us)
Async XLA Ops:
  6.5 15.0 %copy-start = (f32[256,512]{1,0:T(8,128)S(1)}, f32[256,512]{1,0:T(8,128)}, u32[]{:S(2)}) copy-start(f32[256,512]{1,0:T(8,128)} %param.1) | copy-start | bytes 1572868
  6.5 387.3 %all-reduce.12.cloned.1.call-start = ((), (), s32[]{:S(2)}) async-start(), calls=%async_computation | async-start | bytes 6684672
  7.7 10.1 %collective-permute-start = (f32[256,64]{1,0:T(8,128)S(1)}, f32[256,64]{1,0:T(8,128)S(1)}, u32[]{:S(2)}, u32[]{:S(2)}) collective-permute-start(f32[256,64]{1,0:T(8,128)S(1)} %get-tuple-element.13), channel_id=1, source_target_pairs={{0,1},{1,2},{2,3},{3,4},{4,5},{5,6},{6,7},{7,8},{8,9},{9,10},{10,1... | collective-permute-start | bytes 196616 | tf_op jit(solution)/shard_map/ppermute | solution.py:21
  13.7 7.8 %collective-permute-start.1 = (f32[256,64]{1,0:T(8,128)S(1)}, f32[256,64]{1,0:T(8,128)S(1)}, u32[]{:S(2)}, u32[]{:S(2)}) collective-permute-start(f32[256,64]{1,0:T(8,128)S(1)} %get-tuple-element.14), channel_id=1, source_target_pairs={{1,0},{2,1},{3,2},{4,3},{5,4},{6,5},{7,6},{8,7},{9,8},{10,9},{11,1... | collective-permute-start | bytes 196616 | tf_op jit(solution)/shard_map/ppermute | solution.py:22
  40.1 15.5 %collective-permute-start.6 = (bf16[256,512]{1,0:T(8,128)(2,1)S(1)}, bf16[256,512]{1,0:T(8,128)(2,1)S(1)}, u32[]{:S(2)}, u32[]{:S(2)}) collective-permute-start(bf16[256,512]{1,0:T(8,128)(2,1)S(1)} %divide_convert_fusion), channel_id=1, source_target_pairs={{32,0},{64,32},{96,64},{128,96},{160,128},{192,160},{224,192},{256... | collective-permute-start | bytes 786440 | tf_op jit(solution)/shard_map/ppermute | solution.py:30
  50.8 12.9 %collective-permute-start.2 = (bf16[256,512]{1,0:T(8,128)(2,1)S(1)}, bf16[256,512]{1,0:T(8,128)(2,1)S(1)}, u32[]{:S(2)}, u32[]{:S(2)}) collective-permute-start(bf16[256,512]{1,0:T(8,128)(2,1)S(1)} %divide_convert_fusion), channel_id=1, source_target_pairs={{480,0},{0,32},{32,64},{64,96},{96,128},{128,160},{160,192},{192,2... | collective-permute-start | bytes 786440 | tf_op jit(solution)/shard_map/ppermute | solution.py:30
  55.6 14.0 %collective-permute-start.7 = (bf16[256,512]{1,0:T(8,128)(2,1)S(1)}, bf16[256,512]{1,0:T(8,128)(2,1)S(1)}, u32[]{:S(2)}, u32[]{:S(2)}) collective-permute-start(bf16[256,512]{1,0:T(8,128)(2,1)S(1)} %collective-permute-done.6), channel_id=1, source_target_pairs={{32,0},{64,32},{96,64},{128,96},{160,128},{192,160},{224,192},{256... | collective-permute-start | bytes 786440 | tf_op jit(solution)/shard_map/ppermute | solution.py:30
  63.7 14.8 %collective-permute-start.3 = (bf16[256,512]{1,0:T(8,128)(2,1)S(1)}, bf16[256,512]{1,0:T(8,128)(2,1)S(1)}, u32[]{:S(2)}, u32[]{:S(2)}) collective-permute-start(bf16[256,512]{1,0:T(8,128)(2,1)S(1)} %collective-permute-done.2), channel_id=1, source_target_pairs={{480,0},{0,32},{32,64},{64,96},{96,128},{128,160},{160,192},{192,2... | collective-permute-start | bytes 786440 | tf_op jit(solution)/shard_map/ppermute | solution.py:30
  69.6 14.7 %collective-permute-start.8 = (bf16[256,512]{1,0:T(8,128)(2,1)S(1)}, bf16[256,512]{1,0:T(8,128)(2,1)S(1)}, u32[]{:S(2)}, u32[]{:S(2)}) collective-permute-start(bf16[256,512]{1,0:T(8,128)(2,1)S(1)} %collective-permute-done.7), channel_id=1, source_target_pairs={{32,0},{64,32},{96,64},{128,96},{160,128},{192,160},{224,192},{256... | collective-permute-start | bytes 786440 | tf_op jit(solution)/shard_map/ppermute | solution.py:30
  78.8 13.9 %collective-permute-start.4 = (bf16[256,512]{1,0:T(8,128)(2,1)S(1)}, bf16[256,512]{1,0:T(8,128)(2,1)S(1)}, u32[]{:S(2)}, u32[]{:S(2)}) collective-permute-start(bf16[256,512]{1,0:T(8,128)(2,1)S(1)} %collective-permute-done.3), channel_id=1, source_target_pairs={{480,0},{0,32},{32,64},{64,96},{96,128},{128,160},{160,192},{192,2... | collective-permute-start | bytes 786440 | tf_op jit(solution)/shard_map/ppermute | solution.py:30
  84.3 14.0 %collective-permute-start.9 = (bf16[256,512]{1,0:T(8,128)(2,1)S(1)}, bf16[256,512]{1,0:T(8,128)(2,1)}, u32[]{:S(2)}, u32[]{:S(2)}) collective-permute-start(bf16[256,512]{1,0:T(8,128)(2,1)S(1)} %collective-permute-done.8), channel_id=1, source_target_pairs={{32,0},{64,32},{96,64},{128,96},{160,128},{192,160},{224,192},{256... | collective-permute-start | bytes 786440 | tf_op jit(solution)/shard_map/ppermute | solution.py:30
  92.7 9.2 %collective-permute-start.5 = (bf16[256,512]{1,0:T(8,128)(2,1)S(1)}, bf16[256,512]{1,0:T(8,128)(2,1)S(1)}, u32[]{:S(2)}, u32[]{:S(2)}) collective-permute-start(bf16[256,512]{1,0:T(8,128)(2,1)S(1)} %collective-permute-done.4), channel_id=1, source_target_pairs={{480,0},{0,32},{32,64},{64,96},{96,128},{128,160},{160,192},{192,2... | collective-permute-start | bytes 786440 | tf_op jit(solution)/shard_map/ppermute | solution.py:30
Sparse Core Ops, SparseCore 0:
  104.1 289.7 all-reduce.11
where the time goes:
time: 409 us; the launch traced here: 408 us
  waiting for transfers between devices  292 us (71%)
  starting transfers between devices  53.5 us (13%)
  local copies, waits for them, and re-layouts  25.5 us (6%)
  other arithmetic  18.1 us (4%)
  between operations  14.8 us (4%)
    unnamed x2, waiting for transfers between devices  288 us
    ppermute x8, starting transfers between devices, passed_along(): return lax.ppermute(block, axis, route)  43.4 us
    another operation x1, other arithmetic, running_level(): lax.reduce_window(magnitude, jnp.zeros((), jnp.float32), lax.add, (1, 2 *...  17.7 us
    reshape x8, local copies, waits for them, and re-layouts, correlate(): return (product * stack_scale).reshape(SRC, receivers.shape[0] * LAGS)  10.3 us
  transfers between devices with their start and end apart: 11, of which 3 were waited for; matrix products, arithmetic and copies ran while one was open for 4% of the time, Pallas kernels for 0%

commit v1 on v0

v1 whole, which is shorter than its diff:
```python
import functools

import jax
import jax.numpy as jnp
from jax import lax
from jax.experimental import pallas as pl
from jax.experimental.pallas import tpu as pltpu
from jax.sharding import PartitionSpec as P

SRC = 8
MAXLAG = 25
LAGS = 51
W2 = 64
EDGE = 128
HALF = 26
SLOT = 640
MEMBERS = 2
CHUNKS = ((0, 7), (7, 13))
MESH = pl.DeviceIdType.MESH


def split(value):
    high = value.astype(jnp.bfloat16)
    low = (value - high.astype(jnp.float32)).astype(jnp.bfloat16)
    return high, low


def correlate_kernel(
    sizes, x_hbm, out_ref,
    own, halo, normed, pieces, pieces_in, mine, sources_in, lagged, padded, partial,
    partial_in, sums, stacked,
    load_sem, halo_s, halo_r, piece_s, piece_r, src_s, src_r, part_s, part_r, sum_s, sum_r,
):
    n_chan, n_tm = sizes
    rows, length = own.shape
    members = MEMBERS
    groups = n_tm // members
    reach = 4
    offsets = [d for d in range(-reach, reach + 1) if d != 0]
    n_off = len(offsets)
    chan = lax.axis_index("chan")
    tm = lax.axis_index("tm")
    group = tm // members
    member = tm % members

    def chan_at(d):
        return lax.rem(chan + d + n_chan, n_chan)

    def tm_at(d):
        return lax.rem(tm + d + n_tm, n_tm)

    def mate(delta):
        return group * members + lax.rem(member + delta, members)

    def cousin(delta):
        return lax.rem(group + delta, groups) * members + member

    load = pltpu.make_async_copy(x_hbm, own, load_sem)
    load.start()

    barrier = pltpu.get_barrier_semaphore()

    def greet(c, t):
        pl.semaphore_signal(barrier, inc=1, device_id=(c, t), device_id_type=MESH)

    greet(chan, tm_at(1))
    greet(chan, tm_at(-1))
    for delta in range(1, members):
        greet(chan, mate(delta))
    for d in offsets:
        for delta in range(members):
            greet(chan_at(d), mate(delta))

    def greet_cousin(delta, carry):
        greet(chan, cousin(delta))
        return carry

    lax.fori_loop(1, groups, greet_cousin, 0)
    pl.semaphore_wait(barrier, 2 + members - 1 + n_off * members + groups - 1)

    def send(src, dst, s, r, c, t):
        return pltpu.make_async_remote_copy(
            src_ref=src, dst_ref=dst, send_sem=s, recv_sem=r,
            device_id=(c, t), device_id_type=MESH,
        )

    to_right = send(x_hbm.at[:, pl.ds(length - EDGE, EDGE)], halo.at[0], halo_s.at[0], halo_r.at[0], chan, tm_at(1))
    to_left = send(x_hbm.at[:, pl.ds(0, EDGE)], halo.at[1], halo_s.at[1], halo_r.at[1], chan, tm_at(-1))
    to_right.start()
    to_left.start()
    load.wait()

    row = lax.broadcasted_iota(jnp.int32, (512, 256), 0)
    col = lax.broadcasted_iota(jnp.int32, (512, 256), 1)
    band = (jnp.abs(row - EDGE - col) <= W2).astype(jnp.float32).astype(jnp.bfloat16)
    value = own[...]
    to_right.wait_recv()
    to_left.wait_recv()
    left = jnp.abs(halo[0]) * (tm > 0).astype(jnp.float32)
    right = jnp.abs(halo[1]) * (tm < n_tm - 1).astype(jnp.float32)
    magnitude = jnp.concatenate([left, jnp.abs(value), right], axis=1)
    high, low = split(magnitude)
    both = jnp.concatenate([high, low], axis=0)
    for part in range(length // 256):
        window = both[:, part * 256 : part * 256 + 512]
        total = jnp.dot(window, band, preferred_element_type=jnp.float32)
        level = (total[:rows] + total[rows:]) / (2 * W2 + 1) + 1e-05
        here = slice(part * 256, part * 256 + 256)
        normed[:, here] = (value[:, here] / level).astype(jnp.bfloat16).astype(jnp.float32)

    picked = jnp.concatenate([normed[pl.ds(q * (rows // SRC), 1), :] for q in range(SRC)], axis=0)
    mine[...] = jnp.concatenate([picked[:, :256], picked[:, 256:]], axis=0).astype(jnp.bfloat16)
    source_sends = []
    for o, d in enumerate(offsets):
        for delta in range(members):
            slot = (members - delta) % members
            source_sends.append(send(mine, sources_in.at[slot, o], src_s.at[slot, o], src_r.at[slot, o], chan_at(d), mate(delta)))
            source_sends[-1].start()

    for m in range(members):
        for pair in range(groups // 2):
            first = (2 * pair * members + m) * 8
            second = ((2 * pair + 1) * members + m) * 8
            block = jnp.concatenate([normed[pl.ds(first, 8), :], normed[pl.ds(second, 8), :]], axis=0)
            pieces[m, pl.ds(pair * 16, 16), :] = block.astype(jnp.bfloat16)
    piece_sends = []
    for delta in range(1, members):
        slot = members - delta
        target = lax.rem(member + delta, members)
        piece_sends.append(send(pieces.at[target], pieces_in.at[slot - 1], piece_s.at[slot - 1], piece_r.at[slot - 1], chan, mate(delta)))
        piece_sends[-1].start()

    count = rows // members
    blank = jnp.zeros((count, SLOT - length), jnp.float32)

    def place(slot, block):
        wide = jnp.concatenate([block.astype(jnp.float32), blank], axis=1)
        late = pltpu.roll(wide, HALF, 1)
        pair = jnp.concatenate([wide.reshape(groups, 8, SLOT), late.reshape(groups, 8, SLOT)], axis=1)
        lagged[:, pl.ds(slot * SLOT, SLOT)] = pair.reshape(groups * 16, SLOT).astype(jnp.bfloat16)

    place(0, pieces[member])
    for copy in piece_sends:
        copy.wait_recv()
    for slot in range(1, members):
        place(slot, pieces_in[slot - 1])
    for copy in source_sends:
        copy.wait_recv()
    n_src = n_off * SRC
    for slot in range(members):
        block = sources_in[slot].astype(jnp.float32)
        joined = jnp.concatenate([block[:, :SRC, :], block[:, SRC:, :]], axis=2).reshape(n_src, length)
        padded[:, pl.ds(slot * SLOT, SLOT)] = jnp.concatenate(
            [joined, jnp.zeros((n_src, SLOT - length), jnp.float32)], axis=1
        )

    scale = 1.0 / float(length * n_tm) ** 0.5

    def start_partials(chunk):
        first, last = CHUNKS[chunk]
        lanes = pl.ds(first * 128, (last - first) * 128)

        def one(delta, carry):
            to = lax.rem(group + delta, groups)
            send(
                partial.at[to, :, lanes], partial_in.at[delta - 1, :, lanes],
                part_s.at[chunk, delta - 1], part_r.at[chunk, delta - 1], chan, to * members + member,
            ).start()
            return carry

        lax.fori_loop(1, groups, one, 0)

    for chunk, (first, last) in enumerate(CHUNKS):
        for tile in range(first, last):
            wide = padded[...]
            shifted = jnp.concatenate(
                [pltpu.roll(wide, 2 * tile, 1) if tile else wide, pltpu.roll(wide, 2 * tile + 1, 1)], axis=0
            ).astype(jnp.bfloat16)
            product = lax.dot_general(
                lagged[...], shifted, (((1,), (1,)), ((), ())), preferred_element_type=jnp.float32
            )
            partial[:, :, tile * 128 : tile * 128 + 128] = (product * scale).astype(jnp.bfloat16).reshape(groups, 16, 128)
        start_partials(chunk)

    tall = 512
    k = lax.broadcasted_iota(jnp.int32, (tall, tall), 0)
    j = lax.broadcasted_iota(jnp.int32, (tall, tall), 1)
    b = jnp.bitwise_and(k, 7)
    late = jnp.bitwise_and(jnp.right_shift(k, 3), 1)
    tile = jnp.bitwise_and(jnp.right_shift(k, 4), 15)
    shift = 2 * tile + jnp.right_shift(k, 8)
    lag = shift - HALF * late + MAXLAG
    target = b * LAGS + lag
    fits = jnp.logical_and(jnp.logical_and(lag >= 0, tile < 13), target == j)
    order = fits.astype(jnp.float32).astype(jnp.bfloat16)

    def await_partials(delta, carry):
        for chunk, (first, last) in enumerate(CHUNKS):
            lanes = pl.ds(first * 128, (last - first) * 128)
            send(
                partial.at[0, :, lanes], partial_in.at[delta - 1, :, lanes],
                part_s.at[chunk, delta - 1], part_r.at[chunk, delta - 1], chan, cousin(delta),
            ).wait()
        return carry

    lax.fori_loop(1, groups, await_partials, 0)
    total = partial[group].astype(jnp.float32)
    for delta in range(1, groups):
        total = total + partial_in[delta - 1].astype(jnp.float32)
    tiles = [total[:, t * 128 : t * 128 + 128] for t in range(13)]
    tiles.append(jnp.zeros((48, 128), jnp.float32))
    turned = jnp.concatenate(tiles, axis=0).T
    flat = jnp.concatenate([turned[:n_src], turned[n_src:]], axis=1)
    high, low = split(flat)
    moved = jnp.dot(jnp.concatenate([high, low], axis=0), order, preferred_element_type=jnp.float32)
    sums[...] = moved[:n_src] + moved[n_src:]

    sum_sends = []
    for o, d in enumerate(offsets):
        part = pl.ds(o * SRC, SRC)
        sum_sends.append(send(sums.at[part, :], stacked.at[part, :], sum_s.at[o], sum_r.at[o], chan_at(-d), tm))
        sum_sends[-1].start()
    for copy in sum_sends:
        copy.wait_recv()
    out_ref[...] = stacked[...].reshape(n_off, SRC, 512)

    to_right.wait_send()
    to_left.wait_send()
    for copy in source_sends + piece_sends + sum_sends:
        copy.wait_send()


def body(sizes, strain_rate):
    rows, length = strain_rate.shape
    n_chan, n_tm = sizes
    members = MEMBERS
    groups = n_tm // members
    n_off = 8
    f32, bf16 = jnp.float32, jnp.bfloat16
    dma = pltpu.SemaphoreType.DMA
    stacks = pl.pallas_call(
        functools.partial(correlate_kernel, sizes),
        out_shape=jax.ShapeDtypeStruct((n_off, SRC, 512), f32),
        in_specs=[pl.BlockSpec(memory_space=pl.ANY)],
        out_specs=pl.BlockSpec(memory_space=pltpu.VMEM),
        scratch_shapes=[
            pltpu.VMEM((rows, length), f32),
            pltpu.VMEM((2, rows, EDGE), f32),
            pltpu.VMEM((rows, length), f32),
            pltpu.VMEM((members, rows // members, length), bf16),
            pltpu.VMEM((members - 1, rows // members, length), bf16),
            pltpu.VMEM((2 * SRC, length // 2), bf16),
            pltpu.VMEM((members, n_off, 2 * SRC, length // 2), bf16),
            pltpu.VMEM((groups * 16, members * SLOT), bf16),
            pltpu.VMEM((n_off * SRC, members * SLOT), f32),
            pltpu.VMEM((groups, 16, 13 * 128), bf16),
            pltpu.VMEM((groups - 1, 16, 13 * 128), bf16),
            pltpu.VMEM((n_off * SRC, 512), f32),
            pltpu.VMEM((n_off * SRC, 512), f32),
            dma, dma((2,)), dma((2,)), dma((members - 1,)), dma((members - 1,)),
            dma((members, n_off)), dma((members, n_off)),
            dma((len(CHUNKS), groups - 1)), dma((len(CHUNKS), groups - 1)),
            dma((n_off,)), dma((n_off,)),
        ],
        compiler_params=pltpu.CompilerParams(
            collective_id=0, has_side_effects=True, vmem_limit_bytes=48 * 1024 * 1024
        ),
    )(strain_rate)
    return jnp.transpose(stacks[:, :, : (rows // n_tm) * LAGS], (1, 0, 2))


def solution(mesh):
    sizes = (mesh.shape["chan"], mesh.shape["tm"])
    return jax.shard_map(
        functools.partial(body, sizes), mesh=mesh, in_specs=(P("chan", "tm"),),
        out_specs=P("chan", None, "tm"), check_vma=False,
    )
```

time: 409 us -> 57 us (0.14)
  waiting for transfers between devices: 292 us -> 0 us
  Pallas kernels: 0 us -> 54.4 us
  starting transfers between devices: 53.5 us -> 0 us
  local copies, waits for them, and re-layouts: 25.5 us -> 1.79 us
  other arithmetic: 18.1 us -> 0 us
  between operations: 14.8 us -> 0.02 us
    unnamed x2 -> x0, waiting for transfers between devices: 288 us -> none
    pallas_call x0 -> x1, Pallas kernels: none -> 54.4 us  [body(): pl.pallas_call(functools.partial(correlate_kernel, sizes), out_shape=jax....]
    ppermute x10 -> x0, starting transfers between devices: 53.5 us -> none  [the longest x8 43.4 us: passed_along(): return lax.ppermute(block, axis, route)]
    another operation x1 -> x0, other arithmetic: 17.7 us -> none  [running_level(): lax.reduce_window(magnitude, jnp.zeros((), jnp.float32), lax.add, (1, 2 *...]
    reshape x8 -> x0, local copies, waits for them, and re-layouts: 10.3 us -> none  [correlate(): return (product * stack_scale).reshape(SRC, receivers.shape[0] * LAGS)]
    unnamed x10 -> x2, local copies, waits for them, and re-layouts: 6.88 us -> 1.04 us
    ppermute x10 -> x0, waiting for transfers between devices: 4.5 us -> none  [the longest x1 3.73 us: with_halo(): after = lax.ppermute(first, axis, down)]
    another operation x58 -> x0, local copies, waits for them, and re-layouts: 4.15 us -> none  [the longest x55 2.42 us: lag_rows(): jnp.stack([padded[:, 2 * MAXLAG - position:2 * MAXLAG - position + shard_...]
  transfers between devices with their start and end apart: 11 -> 0, of which waited for: 3 -> 0; matrix products, arithmetic and copies ran while one was open for 4% -> 0% of each run, Pallas kernels for 0% -> 0%
where the time goes in v1:
time: 57 us; the launch traced here: 56.2 us
  Pallas kernels  54.4 us (95%)
  local copies, waits for them, and re-layouts  1.79 us (3%)
    pallas_call x1, Pallas kernels, body(): pl.pallas_call(functools.partial(correlate_kernel, sizes), out_shape=jax....  54.4 us

profile of v1, /device:TPU:1, one launch (start us, length us, event | category | flops | bytes accessed | tf_op | source)
XLA Modules:
  0.0 56.2 jit_solution(5451666987038199031)
XLA Ops:
  0.0 0.0 copy-start
  0.0 1.0 %copy-done = f32[256,512]{1,0:T(8,128)S(1)} copy-done((f32[256,512]{1,0:T(8,128)S(1)}, f32[256,512]{1,0:T(8,128)}, u32[]{:S(2)}) %copy-start) | copy-done | bytes 524312
  1.0 54.4 %shard_map.17 = f32[8,8,512]{2,1,0:T(8,128)S(1)} custom-call(f32[256,512]{1,0:T(8,128)S(1)} %copy-done), custom_call_target="tpu_custom_call" | custom-call | tf_op jit(solution)/shard_map/pallas_call | solution.py:241
  55.5 0.7 %copy.2 = f32[8,8,408]{2,1,0:T(8,128)} copy(f32[8,8,408]{2,0,1:T(8,128)S(1)} %slice_bitcast_fusion) | data formatting | bytes 208896 | tf_op jit(solution)/shard_map/transpose | solution.py:269
  (1 shorter events, 0.0 us)
Async XLA Ops:
  0.0 1.0 %copy-start = (f32[256,512]{1,0:T(8,128)S(1)}, f32[256,512]{1,0:T(8,128)}, u32[]{:S(2)}) copy-start(f32[256,512]{1,0:T(8,128)} %x_hbm.1) | copy-start | bytes 1572868

commit v2 on v1

v2 whole, which is shorter than its diff:
```python
import functools

import jax
import jax.numpy as jnp
from jax import lax
from jax.experimental import pallas as pl
from jax.experimental.pallas import tpu as pltpu
from jax.sharding import PartitionSpec as P

SRC = 8
MAXLAG = 25
LAGS = 51
W2 = 64
EDGE = 128
LATE = 26
SLOT = 640
REACH = 4
OFFSETS = [d for d in range(-REACH, REACH + 1) if d != 0]
TILES = 13
FAR_FIRST = (4, 3, 5, 2, 6, 1, 7)
CHUNKS = ((0, 4), (4, 8), (8, 13))
MESH = pl.DeviceIdType.MESH


def split(value):
    high = value.astype(jnp.bfloat16)
    low = (value - high.astype(jnp.float32)).astype(jnp.bfloat16)
    return high, low


def correlate_kernel(
    sizes, x_hbm, out_ref,
    own, edges, halo, normed, pieces, pieces_in, mine, sources_in, lagged, padded, partial,
    partial_in, sums, stacked,
    load_sem, ready, halo_s, halo_r, piece_s, piece_r, src_s, src_r, part_s, part_r, sum_s, sum_r,
):
    n_chan, n_tm = sizes
    rows, length = own.shape
    groups = n_tm // 4
    chan = lax.axis_index("chan")
    tm = lax.axis_index("tm")
    group, pair, core = tm // 4, (tm // 2) % 2, tm % 2

    def chan_at(d):
        return lax.rem(chan + d + n_chan, n_chan)

    def tm_at(d):
        return lax.rem(tm + d + n_tm, n_tm)

    def mate(across, other):
        return group * 4 + lax.rem(pair + across, 2) * 2 + lax.rem(core + other, 2)

    def cousin(delta):
        return lax.rem(group + delta, groups) * 4 + pair * 2 + core

    mates = ((0, 1), (1, 0), (1, 1))

    load = pltpu.make_async_copy(x_hbm, own, load_sem)
    load.start()

    barrier = pltpu.get_barrier_semaphore()

    def greet(c, t):
        pl.semaphore_signal(barrier, inc=1, device_id=(c, t), device_id_type=MESH)

    greet(chan, tm_at(1))
    greet(chan, tm_at(-1))
    for d in OFFSETS:
        greet(chan_at(d), tm)
    for across, other in mates:
        greet(chan, mate(across, other))
    for delta in range(1, groups):
        greet(chan, cousin(delta))

    load.wait()
    value = own[...]
    half = rows // 2
    lane = lax.broadcasted_iota(jnp.int32, (half, EDGE), 1)
    first_edge = jnp.abs(value[:, :EDGE])
    last_edge = jnp.abs(value[:, length - EDGE :])
    edges[0] = jnp.where(lane < W2, pltpu.roll(last_edge[:half], W2, 1), last_edge[half:]).astype(jnp.bfloat16)
    edges[1] = jnp.where(lane < W2, first_edge[:half], pltpu.roll(first_edge[half:], W2, 1)).astype(jnp.bfloat16)
    row = lax.broadcasted_iota(jnp.int32, (512, 256), 0)
    col = lax.broadcasted_iota(jnp.int32, (512, 256), 1)
    band = (jnp.abs(row - EDGE - col) <= W2).astype(jnp.float32).astype(jnp.bfloat16)

    pl.semaphore_wait(barrier, 2 + len(OFFSETS) + len(mates) + groups - 1)

    def send(src, dst, s, r, c, t):
        return pltpu.make_async_remote_copy(
            src_ref=src, dst_ref=dst, send_sem=s, recv_sem=r,
            device_id=(c, t), device_id_type=MESH,
        )

    to_right = send(edges.at[0], halo.at[0], halo_s.at[0], halo_r.at[0], chan, tm_at(1))
    to_left = send(edges.at[1], halo.at[1], halo_s.at[1], halo_r.at[1], chan, tm_at(-1))
    to_right.start()
    to_left.start()
    for across, other in mates:
        pl.semaphore_signal(ready, inc=1, device_id=(chan, mate(across, other)), device_id_type=MESH)

    to_right.wait_recv()
    to_left.wait_recv()
    before = halo[0].astype(jnp.float32) * (tm > 0).astype(jnp.float32)
    after = halo[1].astype(jnp.float32) * (tm < n_tm - 1).astype(jnp.float32)
    left = jnp.concatenate([pltpu.roll(before, W2, 1), before], axis=0)
    right = jnp.concatenate([after, pltpu.roll(after, W2, 1)], axis=0)
    magnitude = jnp.concatenate([left, jnp.abs(value), right], axis=1)
    high, low = split(magnitude)
    both = jnp.concatenate([high, low], axis=0)
    for part in range(length // 256):
        window = both[:, part * 256 : part * 256 + 512]
        total = jnp.dot(window, band, preferred_element_type=jnp.float32)
        level = (total[:rows] + total[rows:]) / (2 * W2 + 1) + 1e-05
        here = slice(part * 256, part * 256 + 256)
        normed[:, here] = (value[:, here] / level).astype(jnp.bfloat16).astype(jnp.float32)

    picked = jnp.concatenate([normed[pl.ds(q * (rows // SRC), 1), :] for q in range(SRC)], axis=0)
    mine[...] = jnp.concatenate([picked[:, :256], picked[:, 256:]], axis=0).astype(jnp.bfloat16)
    source_sends = []
    pl.semaphore_wait(ready, len(mates))
    for across in range(2):
        for o, d in enumerate(OFFSETS):
            side, place_o = o // REACH, o % REACH
            slot = across * 2 + lax.rem(core + side, 2)
            to = group * 4 + lax.rem(pair + across, 2) * 2 + side
            source_sends.append(
                send(mine, sources_in.at[slot, place_o], src_s.at[across, o], src_r.at[slot, place_o], chan_at(d), to)
            )
            source_sends[-1].start()

    for p in range(2):
        for g in range(groups):
            pieces[p, pl.ds(g * 16, 16), :] = normed[pl.ds(g * 32 + p * 16, 16), :].astype(jnp.bfloat16)
    def piece_send(src, slot, across, other):
        return send(src, pieces_in.at[slot], piece_s.at[slot], piece_r.at[slot], chan, mate(across, other))

    piece_sends = [
        piece_send(pieces.at[pair], 0, 0, 1),
        piece_send(pieces.at[1 - pair], 1, 1, 0),
        piece_send(pieces_in.at[1], 2, 0, 1),
    ]
    piece_sends[1].start()
    piece_sends[0].start()

    count = groups * 16
    blank = jnp.zeros((count, SLOT - length), jnp.float32)

    def place(slot, block):
        wide = jnp.concatenate([block.astype(jnp.float32), blank], axis=1)
        late = pltpu.roll(wide, LATE, 1)
        two = jnp.concatenate([wide.reshape(groups, 16, SLOT), late.reshape(groups, 16, SLOT)], axis=1)
        lagged[:, slot * SLOT : slot * SLOT + SLOT] = two.reshape(groups * 32, SLOT).astype(jnp.bfloat16)

    place(0, pieces[pair])
    piece_sends[0].wait_recv()
    place(1, pieces_in[0])
    piece_sends[1].wait_recv()
    piece_sends[2].start()
    place(2, pieces_in[1])
    piece_sends[2].wait_recv()
    place(3, pieces_in[2])
    n_src = REACH * SRC
    for slot in range(4):
        for place_o in range(REACH):
            send(mine, sources_in.at[slot, place_o], src_s.at[0, 0], src_r.at[slot, place_o], chan_at(1), tm).wait_recv()
        block = sources_in[slot].astype(jnp.float32)
        joined = jnp.concatenate([block[:, :SRC, :], block[:, SRC:, :]], axis=2).reshape(n_src, length)
        padded[:, slot * SLOT : slot * SLOT + SLOT] = jnp.concatenate(
            [joined, jnp.zeros((n_src, SLOT - length), jnp.float32)], axis=1
        )

    scale = 1.0 / float(length * n_tm) ** 0.5

    def partial_copy(chunk, delta):
        first, last = CHUNKS[chunk]
        to = lax.rem(group + delta, groups)
        part = pl.ds(first, last - first)
        return send(
            partial.at[to, part], partial_in.at[delta - 1, part],
            part_s.at[chunk, delta - 1], part_r.at[chunk, delta - 1], chan, cousin(delta),
        )

    def product(shifts):
        wide = padded[...]
        shifted = jnp.concatenate([pltpu.roll(wide, c, 1) if c else wide for c in shifts], axis=0)
        result = lax.dot_general(
            lagged[...], shifted.astype(jnp.bfloat16), (((1,), (1,)), ((), ())),
            preferred_element_type=jnp.float32,
        )
        return (result * scale).reshape(groups, 2, 16, len(shifts) * n_src)

    for step in range(4):
        if step < 3:
            result = product(range(8 * step, 8 * step + 8)).astype(jnp.bfloat16)
            for late in range(2):
                for side in range(2):
                    partial[:, 4 * step + 2 * late + side] = result[:, late, :, side * 128 : side * 128 + 128]
        else:
            result = product(range(24, 26))
            partial[:, 12] = jnp.concatenate([result[:, 0], result[:, 1]], axis=2).astype(jnp.bfloat16)
        for chunk, (first, last) in enumerate(CHUNKS):
            if last == min(4 * step + 4, TILES):
                for delta in FAR_FIRST:
                    partial_copy(chunk, delta).start()

    tall = 512
    k = lax.broadcasted_iota(jnp.int32, (tall, tall), 0)
    j = lax.broadcasted_iota(jnp.int32, (tall, tall), 1)
    b = jnp.bitwise_and(k, 7)
    tile = jnp.bitwise_and(jnp.right_shift(k, 3), 15)
    quarter = jnp.right_shift(k, 7)
    mixed = tile == 12
    late = jnp.where(mixed, jnp.right_shift(quarter, 1), jnp.bitwise_and(jnp.right_shift(tile, 1), 1))
    shift = jnp.where(
        mixed, 24 + jnp.bitwise_and(quarter, 1),
        8 * jnp.right_shift(tile, 2) + 4 * jnp.bitwise_and(tile, 1) + quarter,
    )
    lag = shift - LATE * late + MAXLAG
    fits = jnp.logical_and(jnp.logical_and(lag >= 0, tile < TILES), b * LAGS + lag == j)
    order = fits.astype(jnp.float32).astype(jnp.bfloat16)

    for chunk in range(len(CHUNKS)):
        for delta in range(1, groups):
            partial_copy(chunk, delta).wait_recv()
    total = partial[group].astype(jnp.float32)
    for delta in range(1, groups):
        total = total + partial_in[delta - 1].astype(jnp.float32)
    spare = jnp.zeros((24, 128), jnp.float32)
    stack = []
    for owner in range(2):
        stack += [total[:, owner * 8 : owner * 8 + 8, :].reshape(TILES * 8, 128), spare]
    turned = jnp.concatenate(stack, axis=0).T
    flat = jnp.concatenate(
        [
            jnp.concatenate(
                [turned[n_src * s : n_src * s + n_src, owner * 128 : owner * 128 + 128] for s in range(4)], axis=1
            )
            for owner in range(2)
        ],
        axis=0,
    )
    high, low = split(flat)
    moved = jnp.dot(jnp.concatenate([high, low], axis=0), order, preferred_element_type=jnp.float32)
    sums[...] = moved[: 2 * n_src] + moved[2 * n_src :]

    sum_sends = []
    for place_o in range(REACH):
        low_d, high_d = OFFSETS[place_o], OFFSETS[REACH + place_o]
        back = chan_at(-low_d - core * (high_d - low_d))
        for owner in range(2):
            o = core * REACH + place_o
            sum_sends.append(
                send(
                    sums.at[pl.ds((owner * REACH + place_o) * SRC, SRC), :], stacked.at[o],
                    sum_s.at[owner, place_o], sum_r.at[o], back, group * 4 + pair * 2 + owner,
                )
            )
            sum_sends[-1].start()
    for o in range(2 * REACH):
        send(sums.at[pl.ds(0, SRC), :], stacked.at[o], sum_s.at[0, 0], sum_r.at[o], chan_at(1), tm).wait_recv()
    out_ref[...] = stacked[...]

    to_right.wait_send()
    to_left.wait_send()
    for copy in source_sends + piece_sends + sum_sends:
        copy.wait_send()
    for chunk in range(len(CHUNKS)):
        for delta in range(1, groups):
            partial_copy(chunk, delta).wait_send()


def body(sizes, strain_rate):
    rows, length = strain_rate.shape
    n_chan, n_tm = sizes
    groups = n_tm // 4
    n_off = len(OFFSETS)
    f32, bf16 = jnp.float32, jnp.bfloat16
    dma = pltpu.SemaphoreType.DMA
    stacks = pl.pallas_call(
        functools.partial(correlate_kernel, sizes),
        out_shape=jax.ShapeDtypeStruct((n_off, SRC, 512), f32),
        in_specs=[pl.BlockSpec(memory_space=pl.ANY)],
        out_specs=pl.BlockSpec(memory_space=pltpu.VMEM),
        scratch_shapes=[
            pltpu.VMEM((rows, length), f32),
            pltpu.VMEM((2, rows // 2, EDGE), bf16),
            pltpu.VMEM((2, rows // 2, EDGE), bf16),
            pltpu.VMEM((rows, length), f32),
            pltpu.VMEM((2, rows // 2, length), bf16),
            pltpu.VMEM((3, rows // 2, length), bf16),
            pltpu.VMEM((2 * SRC, length // 2), bf16),
            pltpu.VMEM((4, REACH, 2 * SRC, length // 2), bf16),
            pltpu.VMEM((groups * 32, 4 * SLOT), bf16),
            pltpu.VMEM((REACH * SRC, 4 * SLOT), f32),
            pltpu.VMEM((groups, TILES, 16, 128), bf16),
            pltpu.VMEM((groups - 1, TILES, 16, 128), bf16),
            pltpu.VMEM((2 * REACH * SRC, 512), f32),
            pltpu.VMEM((n_off, SRC, 512), f32),
            dma, pltpu.SemaphoreType.REGULAR, dma((2,)), dma((2,)), dma((3,)), dma((3,)),
            dma((2, n_off)), dma((4, REACH)),
            dma((len(CHUNKS), groups - 1)), dma((len(CHUNKS), groups - 1)),
            dma((2, REACH)), dma((n_off,)),
        ],
        compiler_params=pltpu.CompilerParams(
            collective_id=0, has_side_effects=True, vmem_limit_bytes=48 * 1024 * 1024
        ),
    )(strain_rate)
    return jnp.transpose(stacks[:, :, : (rows // n_tm) * LAGS], (1, 0, 2))


def solution(mesh):
    sizes = (mesh.shape["chan"], mesh.shape["tm"])
    return jax.shard_map(
        functools.partial(body, sizes), mesh=mesh, in_specs=(P("chan", "tm"),),
        out_specs=P("chan", None, "tm"), check_vma=False,
    )
```

time: 57 us -> 48.3 us (0.85); the launches traced: 56.2 us -> 48.1 us
  Pallas kernels: 54.4 us -> 46.3 us
    pallas_call x1, Pallas kernels: 54.4 us -> 46.3 us  [body(): pl.pallas_call(functools.partial(correlate_kernel, sizes), out_shape=jax....]
where the time goes in v2:
time: 48.3 us; the launch traced here: 48.1 us
  Pallas kernels  46.3 us (96%)
  local copies, waits for them, and re-layouts  1.79 us (4%)
    pallas_call x1, Pallas kernels, body(): pl.pallas_call(functools.partial(correlate_kernel, sizes), out_shape=jax....  46.3 us
    unnamed x2, local copies, waits for them, and re-layouts  1.04 us

profile of v2, /device:TPU:1, one launch (start us, length us, event | category | flops | bytes accessed | tf_op | source)
XLA Modules:
  0.0 48.1 jit_solution(3881624840748917185)
XLA Ops:
  0.0 0.0 copy-start
  0.0 1.0 %copy-done = f32[256,512]{1,0:T(8,128)S(1)} copy-done((f32[256,512]{1,0:T(8,128)S(1)}, f32[256,512]{1,0:T(8,128)}, u32[]{:S(2)}) %copy-start) | copy-done | bytes 524312
  1.0 46.3 %shard_map.17 = f32[8,8,512]{2,1,0:T(8,128)S(1)} custom-call(f32[256,512]{1,0:T(8,128)S(1)} %copy-done), custom_call_target="tpu_custom_call" | custom-call | tf_op jit(solution)/shard_map/pallas_call | solution.py:280
  47.4 0.7 %copy.2 = f32[8,8,408]{2,1,0:T(8,128)} copy(f32[8,8,408]{2,0,1:T(8,128)S(1)} %slice_bitcast_fusion) | data formatting | bytes 208896 | tf_op jit(solution)/shard_map/transpose | solution.py:309
  (1 shorter events, 0.0 us)
Async XLA Ops:
  0.0 1.0 %copy-start = (f32[256,512]{1,0:T(8,128)S(1)}, f32[256,512]{1,0:T(8,128)}, u32[]{:S(2)}) copy-start(f32[256,512]{1,0:T(8,128)} %x_hbm.1) | copy-start | bytes 1572868

commit v3 on v2

--- a/solution.py
+++ b/solution.py
@@ -15,7 +15,8 @@
 LATE = 26
 SLOT = 640
 REACH = 4
-OFFSETS = [d for d in range(-REACH, REACH + 1) if d != 0]
+OFFSETS = (-4, 3, -2, 1, 4, -3, 2, -1)
+PLACES = tuple(d + REACH if d < 0 else d + REACH - 1 for d in OFFSETS)
 TILES = 13
 FAR_FIRST = (4, 3, 5, 2, 6, 1, 7)
 CHUNKS = ((0, 4), (4, 8), (8, 13))
@@ -249,7 +250,7 @@
         low_d, high_d = OFFSETS[place_o], OFFSETS[REACH + place_o]
         back = chan_at(-low_d - core * (high_d - low_d))
         for owner in range(2):
-            o = core * REACH + place_o
+            o = PLACES[place_o] + core * (PLACES[REACH + place_o] - PLACES[place_o])
             sum_sends.append(
                 send(
                     sums.at[pl.ds((owner * REACH + place_o) * SRC, SRC), :], stacked.at[o],
@@ -303,7 +304,7 @@
             dma((2, REACH)), dma((n_off,)),
         ],
         compiler_params=pltpu.CompilerParams(
-            collective_id=0, has_side_effects=True, vmem_limit_bytes=48 * 1024 * 1024
+            collective_id=0, has_side_effects=True, vmem_limit_bytes=55000 * 1024
         ),
     )(strain_rate)
     return jnp.transpose(stacks[:, :, : (rows // n_tm) * LAGS], (1, 0, 2))

time: 48.3 us -> 45.8 us (0.948)
  Pallas kernels: 46.3 us -> 44.9 us
  local copies, waits for them, and re-layouts: 1.79 us -> 0.75 us
    pallas_call x1, Pallas kernels: 46.3 us -> 44.9 us  [body(): pl.pallas_call(functools.partial(correlate_kernel, sizes), out_shape=jax....]
    unnamed x2 -> x0, local copies, waits for them, and re-layouts: 1.04 us -> none
where the time goes in v3:
time: 45.8 us; the launch traced here: 45.7 us
  Pallas kernels  44.9 us (98%)
  local copies, waits for them, and re-layouts  0.75 us (2%)
    pallas_call x1, Pallas kernels, body(): pl.pallas_call(functools.partial(correlate_kernel, sizes), out_shape=jax....  44.9 us

profile of v3, /device:TPU:1, one launch (start us, length us, event | category | flops | bytes accessed | tf_op | source)
XLA Modules:
  0.0 45.7 jit_solution(6190211884326631454)
XLA Ops:
  0.0 44.9 %shard_map.17 = f32[8,8,512]{2,1,0:T(8,128)S(1)} custom-call(f32[256,512]{1,0:T(8,128)} %x_hbm.1), custom_call_target="tpu_custom_call" | custom-call | tf_op jit(solution)/shard_map/pallas_call | solution.py:281
  45.0 0.7 %copy.2 = f32[8,8,408]{2,1,0:T(8,128)} copy(f32[8,8,408]{2,0,1:T(8,128)S(1)} %slice_bitcast_fusion) | data formatting | bytes 208896 | tf_op jit(solution)/shard_map/transpose | solution.py:310
  (1 shorter events, 0.0 us)

commit v4 on v3

--- a/solution.py
+++ b/solution.py
@@ -100,21 +100,47 @@
     for across, other in mates:
         pl.semaphore_signal(ready, inc=1, device_id=(chan, mate(across, other)), device_id_type=MESH)
 
+    def normalise(window, here):
+        high, low = split(window)
+        total = jnp.dot(
+            jnp.concatenate([high, low], axis=0), band[: window.shape[1], : here.stop - here.start],
+            preferred_element_type=jnp.float32,
+        )
+        level = (total[:rows] + total[rows:]) / (2 * W2 + 1) + 1e-05
+        normed[:, here] = (value[:, here] / level).astype(jnp.bfloat16).astype(jnp.float32)
+
+    def piece_send(src, kind, slot, across, other):
+        n = 2 * slot + kind
+        return send(src, pieces_in.at[kind, slot], piece_s.at[n], piece_r.at[n], chan, mate(across, other))
+
+    beside = [piece_send(pieces.at[kind, pair], kind, 0, 0, 1) for kind in range(2)]
+    between = [piece_send(pieces.at[kind, 1 - pair], kind, 1, 1, 0) for kind in range(2)]
+    onward = [piece_send(pieces_in.at[kind, 1], kind, 2, 0, 1) for kind in range(2)]
+
+    def give_pieces(kind):
+        for p in range(2):
+            for g in range(groups):
+                at = pl.ds(g * 32 + p * 16, 16)
+                if kind == 0:
+                    block = normed[at, EDGE : length - EDGE]
+                else:
+                    block = jnp.concatenate([normed[at, :EDGE], normed[at, length - EDGE :]], axis=1)
+                pieces[kind, p, pl.ds(g * 16, 16), :] = block.astype(jnp.bfloat16)
+        between[kind].start()
+        beside[kind].start()
+
+    absolute = jnp.abs(value)
+    normalise(absolute, slice(EDGE, length - EDGE))
+    give_pieces(0)
+
     to_right.wait_recv()
     to_left.wait_recv()
     before = halo[0].astype(jnp.float32) * (tm > 0).astype(jnp.float32)
     after = halo[1].astype(jnp.float32) * (tm < n_tm - 1).astype(jnp.float32)
     left = jnp.concatenate([pltpu.roll(before, W2, 1), before], axis=0)
     right = jnp.concatenate([after, pltpu.roll(after, W2, 1)], axis=0)
-    magnitude = jnp.concatenate([left, jnp.abs(value), right], axis=1)
-    high, low = split(magnitude)
-    both = jnp.concatenate([high, low], axis=0)
-    for part in range(length // 256):
-        window = both[:, part * 256 : part * 256 + 512]
-        total = jnp.dot(window, band, preferred_element_type=jnp.float32)
-        level = (total[:rows] + total[rows:]) / (2 * W2 + 1) + 1e-05
-        here = slice(part * 256, part * 256 + 256)
-        normed[:, here] = (value[:, here] / level).astype(jnp.bfloat16).astype(jnp.float32)
+    normalise(jnp.concatenate([left, absolute[:, : 2 * EDGE]], axis=1), slice(0, EDGE))
+    normalise(jnp.concatenate([absolute[:, length - 2 * EDGE :], right], axis=1), slice(length - EDGE, length))
 
     picked = jnp.concatenate([normed[pl.ds(q * (rows // SRC), 1), :] for q in range(SRC)], axis=0)
     mine[...] = jnp.concatenate([picked[:, :256], picked[:, 256:]], axis=0).astype(jnp.bfloat16)
@@ -130,37 +156,27 @@
             )
             source_sends[-1].start()
 
-    for p in range(2):
-        for g in range(groups):
-            pieces[p, pl.ds(g * 16, 16), :] = normed[pl.ds(g * 32 + p * 16, 16), :].astype(jnp.bfloat16)
-    def piece_send(src, slot, across, other):
-        return send(src, pieces_in.at[slot], piece_s.at[slot], piece_r.at[slot], chan, mate(across, other))
-
-    piece_sends = [
-        piece_send(pieces.at[pair], 0, 0, 1),
-        piece_send(pieces.at[1 - pair], 1, 1, 0),
-        piece_send(pieces_in.at[1], 2, 0, 1),
-    ]
-    piece_sends[1].start()
-    piece_sends[0].start()
+    give_pieces(1)
 
     count = groups * 16
     blank = jnp.zeros((count, SLOT - length), jnp.float32)
 
-    def place(slot, block):
-        wide = jnp.concatenate([block.astype(jnp.float32), blank], axis=1)
+    def place(slot, middle, ends):
+        middle, ends = middle.astype(jnp.float32), ends.astype(jnp.float32)
+        wide = jnp.concatenate([ends[:, :EDGE], middle, ends[:, EDGE:], blank], axis=1)
         late = pltpu.roll(wide, LATE, 1)
         two = jnp.concatenate([wide.reshape(groups, 16, SLOT), late.reshape(groups, 16, SLOT)], axis=1)
         lagged[:, slot * SLOT : slot * SLOT + SLOT] = two.reshape(groups * 32, SLOT).astype(jnp.bfloat16)
 
-    place(0, pieces[pair])
-    piece_sends[0].wait_recv()
-    place(1, pieces_in[0])
-    piece_sends[1].wait_recv()
-    piece_sends[2].start()
-    place(2, pieces_in[1])
-    piece_sends[2].wait_recv()
-    place(3, pieces_in[2])
+    between[0].wait_recv()
+    onward[0].start()
+    place(0, pieces[0, pair], pieces[1, pair])
+    for copy in beside:
+        copy.wait_recv()
+    place(1, pieces_in[0, 0], pieces_in[1, 0])
+    between[1].wait_recv()
+    onward[1].start()
+    place(2, pieces_in[0, 1], pieces_in[1, 1])
     n_src = REACH * SRC
     for slot in range(4):
         for place_o in range(REACH):
@@ -170,6 +186,9 @@
         padded[:, slot * SLOT : slot * SLOT + SLOT] = jnp.concatenate(
             [joined, jnp.zeros((n_src, SLOT - length), jnp.float32)], axis=1
         )
+    for copy in onward:
+        copy.wait_recv()
+    place(3, pieces_in[0, 2], pieces_in[1, 2])
 
     scale = 1.0 / float(length * n_tm) ** 0.5
 
@@ -264,7 +283,7 @@
 
     to_right.wait_send()
     to_left.wait_send()
-    for copy in source_sends + piece_sends + sum_sends:
+    for copy in source_sends + beside + between + onward + sum_sends:
         copy.wait_send()
     for chunk in range(len(CHUNKS)):
         for delta in range(1, groups):
@@ -288,8 +307,8 @@
             pltpu.VMEM((2, rows // 2, EDGE), bf16),
             pltpu.VMEM((2, rows // 2, EDGE), bf16),
             pltpu.VMEM((rows, length), f32),
-            pltpu.VMEM((2, rows // 2, length), bf16),
-            pltpu.VMEM((3, rows // 2, length), bf16),
+            pltpu.VMEM((2, 2, rows // 2, length // 2), bf16),
+            pltpu.VMEM((2, 3, rows // 2, length // 2), bf16),
             pltpu.VMEM((2 * SRC, length // 2), bf16),
             pltpu.VMEM((4, REACH, 2 * SRC, length // 2), bf16),
             pltpu.VMEM((groups * 32, 4 * SLOT), bf16),
@@ -298,7 +317,7 @@
             pltpu.VMEM((groups - 1, TILES, 16, 128), bf16),
             pltpu.VMEM((2 * REACH * SRC, 512), f32),
             pltpu.VMEM((n_off, SRC, 512), f32),
-            dma, pltpu.SemaphoreType.REGULAR, dma((2,)), dma((2,)), dma((3,)), dma((3,)),
+            dma, pltpu.SemaphoreType.REGULAR, dma((2,)), dma((2,)), dma((6,)), dma((6,)),
             dma((2, n_off)), dma((4, REACH)),
             dma((len(CHUNKS), groups - 1)), dma((len(CHUNKS), groups - 1)),
             dma((2, REACH)), dma((n_off,)),

time: 45.8 us -> 44.6 us (0.974)
  Pallas kernels: 44.9 us -> 43.7 us
    pallas_call x1, Pallas kernels: 44.9 us -> 43.7 us  [body(): pl.pallas_call(functools.partial(correlate_kernel, sizes), out_shape=jax....]
where the time goes in v4:
time: 44.6 us; the launch traced here: 44.4 us
  Pallas kernels  43.7 us (98%)
  local copies, waits for them, and re-layouts  0.75 us (2%)
    pallas_call x1, Pallas kernels, body(): pl.pallas_call(functools.partial(correlate_kernel, sizes), out_shape=jax....  43.7 us

profile of v4, /device:TPU:1, one launch (start us, length us, event | category | flops | bytes accessed | tf_op | source)
XLA Modules:
  0.0 44.4 jit_solution(3365514356718891171)
XLA Ops:
  0.0 43.7 %shard_map.17 = f32[8,8,512]{2,1,0:T(8,128)S(1)} custom-call(f32[256,512]{1,0:T(8,128)} %x_hbm.1), custom_call_target="tpu_custom_call" | custom-call | tf_op jit(solution)/shard_map/pallas_call | solution.py:300
  43.7 0.7 %copy.2 = f32[8,8,408]{2,1,0:T(8,128)} copy(f32[8,8,408]{2,0,1:T(8,128)S(1)} %slice_bitcast_fusion) | data formatting | bytes 208896 | tf_op jit(solution)/shard_map/transpose | solution.py:329
  (1 shorter events, 0.0 us)

commit v5 on v4

--- a/solution.py
+++ b/solution.py
@@ -129,8 +129,35 @@
         between[kind].start()
         beside[kind].start()
 
+    source_sends = []
+
+    def give_sources(kind):
+        picked = []
+        for q in range(SRC):
+            at = pl.ds(q * (rows // SRC), 1)
+            if kind == 0:
+                picked.append(normed[at, EDGE : length - EDGE])
+            else:
+                picked.append(jnp.concatenate([normed[at, :EDGE], normed[at, length - EDGE :]], axis=1))
+        block = jnp.concatenate(picked, axis=0)
+        mine[kind] = jnp.concatenate([block[:, :EDGE], block[:, EDGE:]], axis=0).astype(jnp.bfloat16)
+        for across in range(2):
+            for o, d in enumerate(OFFSETS):
+                side, place_o = o // REACH, o % REACH
+                slot = across * 2 + lax.rem(core + side, 2)
+                to = group * 4 + lax.rem(pair + across, 2) * 2 + side
+                source_sends.append(
+                    send(
+                        mine.at[kind], sources_in.at[kind, slot, place_o], src_s.at[kind, across, o],
+                        src_r.at[kind, slot, place_o], chan_at(d), to,
+                    )
+                )
+                source_sends[-1].start()
+
     absolute = jnp.abs(value)
     normalise(absolute, slice(EDGE, length - EDGE))
+    pl.semaphore_wait(ready, len(mates))
+    give_sources(0)
     give_pieces(0)
 
     to_right.wait_recv()
@@ -142,21 +169,8 @@
     normalise(jnp.concatenate([left, absolute[:, : 2 * EDGE]], axis=1), slice(0, EDGE))
     normalise(jnp.concatenate([absolute[:, length - 2 * EDGE :], right], axis=1), slice(length - EDGE, length))
 
-    picked = jnp.concatenate([normed[pl.ds(q * (rows // SRC), 1), :] for q in range(SRC)], axis=0)
-    mine[...] = jnp.concatenate([picked[:, :256], picked[:, 256:]], axis=0).astype(jnp.bfloat16)
-    source_sends = []
-    pl.semaphore_wait(ready, len(mates))
-    for across in range(2):
-        for o, d in enumerate(OFFSETS):
-            side, place_o = o // REACH, o % REACH
-            slot = across * 2 + lax.rem(core + side, 2)
-            to = group * 4 + lax.rem(pair + across, 2) * 2 + side
-            source_sends.append(
-                send(mine, sources_in.at[slot, place_o], src_s.at[across, o], src_r.at[slot, place_o], chan_at(d), to)
-            )
-            source_sends[-1].start()
-
     give_pieces(1)
+    give_sources(1)
 
     count = groups * 16
     blank = jnp.zeros((count, SLOT - length), jnp.float32)
@@ -179,10 +193,16 @@
     place(2, pieces_in[0, 1], pieces_in[1, 1])
     n_src = REACH * SRC
     for slot in range(4):
-        for place_o in range(REACH):
-            send(mine, sources_in.at[slot, place_o], src_s.at[0, 0], src_r.at[slot, place_o], chan_at(1), tm).wait_recv()
-        block = sources_in[slot].astype(jnp.float32)
-        joined = jnp.concatenate([block[:, :SRC, :], block[:, SRC:, :]], axis=2).reshape(n_src, length)
+        for kind in range(2):
+            for place_o in range(REACH):
+                send(
+                    mine.at[0], sources_in.at[kind, slot, place_o], src_s.at[0, 0, 0],
+                    src_r.at[kind, slot, place_o], chan_at(1), tm,
+                ).wait_recv()
+        middle, ends = [sources_in[kind, slot].astype(jnp.float32) for kind in range(2)]
+        joined = jnp.concatenate(
+            [ends[:, :SRC], middle[:, :SRC], middle[:, SRC:], ends[:, SRC:]], axis=2
+        ).reshape(n_src, length)
         padded[:, slot * SLOT : slot * SLOT + SLOT] = jnp.concatenate(
             [joined, jnp.zeros((n_src, SLOT - length), jnp.float32)], axis=1
         )
@@ -240,11 +260,10 @@
     fits = jnp.logical_and(jnp.logical_and(lag >= 0, tile < TILES), b * LAGS + lag == j)
     order = fits.astype(jnp.float32).astype(jnp.bfloat16)
 
-    for chunk in range(len(CHUNKS)):
-        for delta in range(1, groups):
+    total = partial[group].astype(jnp.float32)
+    for delta in FAR_FIRST[::-1]:
+        for chunk in range(len(CHUNKS)):
             partial_copy(chunk, delta).wait_recv()
-    total = partial[group].astype(jnp.float32)
-    for delta in range(1, groups):
         total = total + partial_in[delta - 1].astype(jnp.float32)
     spare = jnp.zeros((24, 128), jnp.float32)
     stack = []
@@ -309,8 +328,8 @@
             pltpu.VMEM((rows, length), f32),
             pltpu.VMEM((2, 2, rows // 2, length // 2), bf16),
             pltpu.VMEM((2, 3, rows // 2, length // 2), bf16),
-            pltpu.VMEM((2 * SRC, length // 2), bf16),
-            pltpu.VMEM((4, REACH, 2 * SRC, length // 2), bf16),
+            pltpu.VMEM((2, 2 * SRC, EDGE), bf16),
+            pltpu.VMEM((2, 4, REACH, 2 * SRC, EDGE), bf16),
             pltpu.VMEM((groups * 32, 4 * SLOT), bf16),
             pltpu.VMEM((REACH * SRC, 4 * SLOT), f32),
             pltpu.VMEM((groups, TILES, 16, 128), bf16),
@@ -318,7 +337,7 @@
             pltpu.VMEM((2 * REACH * SRC, 512), f32),
             pltpu.VMEM((n_off, SRC, 512), f32),
             dma, pltpu.SemaphoreType.REGULAR, dma((2,)), dma((2,)), dma((6,)), dma((6,)),
-            dma((2, n_off)), dma((4, REACH)),
+            dma((2, 2, n_off)), dma((2, 4, REACH)),
             dma((len(CHUNKS), groups - 1)), dma((len(CHUNKS), groups - 1)),
             dma((2, REACH)), dma((n_off,)),
         ],

time: 44.6 us -> 43.5 us (0.975)
  Pallas kernels: 43.7 us -> 42.6 us
    pallas_call x1, Pallas kernels: 43.7 us -> 42.6 us  [body(): pl.pallas_call(functools.partial(correlate_kernel, sizes), out_shape=jax....]
where the time goes in v5:
time: 43.5 us; the launch traced here: 43.4 us
  Pallas kernels  42.6 us (98%)
  local copies, waits for them, and re-layouts  0.75 us (2%)
    pallas_call x1, Pallas kernels, body(): pl.pallas_call(functools.partial(correlate_kernel, sizes), out_shape=jax....  42.6 us

profile of v5, /device:TPU:1, one launch (start us, length us, event | category | flops | bytes accessed | tf_op | source)
XLA Modules:
  0.0 43.4 jit_solution(3613877702176008737)
XLA Ops:
  0.0 42.6 %shard_map.17 = f32[8,8,512]{2,1,0:T(8,128)S(1)} custom-call(f32[256,512]{1,0:T(8,128)} %x_hbm.1), custom_call_target="tpu_custom_call" | custom-call | tf_op jit(solution)/shard_map/pallas_call | solution.py:319
  42.6 0.7 %copy.2 = f32[8,8,408]{2,1,0:T(8,128)} copy(f32[8,8,408]{2,0,1:T(8,128)S(1)} %slice_bitcast_fusion) | data formatting | bytes 208896 | tf_op jit(solution)/shard_map/transpose | solution.py:348
  (1 shorter events, 0.0 us)

commit v6 on v5

--- a/solution.py
+++ b/solution.py
@@ -298,7 +298,8 @@
             sum_sends[-1].start()
     for o in range(2 * REACH):
         send(sums.at[pl.ds(0, SRC), :], stacked.at[o], sum_s.at[0, 0], sum_r.at[o], chan_at(1), tm).wait_recv()
-    out_ref[...] = stacked[...]
+    for q in range(SRC):
+        out_ref[q] = stacked[:, q, :][:, : out_ref.shape[2]]
 
     to_right.wait_send()
     to_left.wait_send()
@@ -316,9 +317,9 @@
     n_off = len(OFFSETS)
     f32, bf16 = jnp.float32, jnp.bfloat16
     dma = pltpu.SemaphoreType.DMA
-    stacks = pl.pallas_call(
+    return pl.pallas_call(
         functools.partial(correlate_kernel, sizes),
-        out_shape=jax.ShapeDtypeStruct((n_off, SRC, 512), f32),
+        out_shape=jax.ShapeDtypeStruct((SRC, n_off, (rows // n_tm) * LAGS), f32),
         in_specs=[pl.BlockSpec(memory_space=pl.ANY)],
         out_specs=pl.BlockSpec(memory_space=pltpu.VMEM),
         scratch_shapes=[
@@ -345,7 +346,6 @@
             collective_id=0, has_side_effects=True, vmem_limit_bytes=55000 * 1024
         ),
     )(strain_rate)
-    return jnp.transpose(stacks[:, :, : (rows // n_tm) * LAGS], (1, 0, 2))
 
 
 def solution(mesh):

time: 43.5 us -> 43.5 us (level)
    transpose x2 -> x0, local copies, waits for them, and re-layouts: 0.75 us -> none  [body(): return jnp.transpose(stacks[:, :, :rows // n_tm * LAGS], (1, 0, 2))]
    unnamed x0 -> x1, local copies, waits for them, and re-layouts: none -> 0.66 us
where the time goes in v6:
time: 43.5 us; the launch traced here: 43.3 us
  Pallas kernels  42.6 us (98%)
  local copies, waits for them, and re-layouts  0.66 us (2%)
    pallas_call x1, Pallas kernels, body(): pl.pallas_call(functools.partial(correlate_kernel, sizes), out_shape=jax....  42.6 us

profile of v6, /device:TPU:1, one launch (start us, length us, event | category | flops | bytes accessed | tf_op | source)
XLA Modules:
  0.0 43.3 jit_solution(16477419703249707957)
XLA Ops:
  0.0 42.6 %shard_map.17 = f32[8,8,408]{2,1,0:T(8,128)S(1)} custom-call(f32[256,512]{1,0:T(8,128)} %x_hbm.1), custom_call_target="tpu_custom_call" | custom-call | tf_op jit(solution)/shard_map/pallas_call | solution.py:320
  42.6 0.7 %copy.3 = f32[8,8,408]{2,1,0:T(8,128)} copy(f32[8,8,408]{2,1,0:T(8,128)S(1)} %shard_map.17) | data formatting | bytes 208896

commit v7 on v5

--- a/solution.py
+++ b/solution.py
@@ -85,6 +85,20 @@
     col = lax.broadcasted_iota(jnp.int32, (512, 256), 1)
     band = (jnp.abs(row - EDGE - col) <= W2).astype(jnp.float32).astype(jnp.bfloat16)
 
+    def put(total, here):
+        level = total / (2 * W2 + 1) + 1e-05
+        normed[:, here] = (value[:, here] / level).astype(jnp.bfloat16).astype(jnp.float32)
+
+    def summed(window, weights):
+        total = jnp.dot(window, weights, preferred_element_type=jnp.float32)
+        return total[:rows] + total[rows:]
+
+    high, low = split(jnp.abs(value))
+    both = jnp.concatenate([high, low], axis=0)
+    put(summed(both, band), slice(EDGE, length - EDGE))
+    total_first = summed(both[:, : 2 * EDGE], band[EDGE : 3 * EDGE, :EDGE])
+    total_last = summed(both[:, length - 2 * EDGE :], band[: 2 * EDGE, :EDGE])
+
     pl.semaphore_wait(barrier, 2 + len(OFFSETS) + len(mates) + groups - 1)
 
     def send(src, dst, s, r, c, t):
@@ -99,15 +113,6 @@
     to_left.start()
     for across, other in mates:
         pl.semaphore_signal(ready, inc=1, device_id=(chan, mate(across, other)), device_id_type=MESH)
-
-    def normalise(window, here):
-        high, low = split(window)
-        total = jnp.dot(
-            jnp.concatenate([high, low], axis=0), band[: window.shape[1], : here.stop - here.start],
-            preferred_element_type=jnp.float32,
-        )
-        level = (total[:rows] + total[rows:]) / (2 * W2 + 1) + 1e-05
-        normed[:, here] = (value[:, here] / level).astype(jnp.bfloat16).astype(jnp.float32)
 
     def piece_send(src, kind, slot, across, other):
         n = 2 * slot + kind
@@ -154,8 +159,6 @@
                 )
                 source_sends[-1].start()
 
-    absolute = jnp.abs(value)
-    normalise(absolute, slice(EDGE, length - EDGE))
     pl.semaphore_wait(ready, len(mates))
     give_sources(0)
     give_pieces(0)
@@ -164,10 +167,13 @@
     to_left.wait_recv()
     before = halo[0].astype(jnp.float32) * (tm > 0).astype(jnp.float32)
     after = halo[1].astype(jnp.float32) * (tm < n_tm - 1).astype(jnp.float32)
-    left = jnp.concatenate([pltpu.roll(before, W2, 1), before], axis=0)
-    right = jnp.concatenate([after, pltpu.roll(after, W2, 1)], axis=0)
-    normalise(jnp.concatenate([left, absolute[:, : 2 * EDGE]], axis=1), slice(0, EDGE))
-    normalise(jnp.concatenate([absolute[:, length - 2 * EDGE :], right], axis=1), slice(length - EDGE, length))
+    left = jnp.concatenate([pltpu.roll(before, W2, 1), before], axis=0).astype(jnp.bfloat16)
+    right = jnp.concatenate([after, pltpu.roll(after, W2, 1)], axis=0).astype(jnp.bfloat16)
+    put(total_first + jnp.dot(left, band[:EDGE, :EDGE], preferred_element_type=jnp.float32), slice(0, EDGE))
+    put(
+        total_last + jnp.dot(right, band[2 * EDGE : 3 * EDGE, :EDGE], preferred_element_type=jnp.float32),
+        slice(length - EDGE, length),
+    )
 
     give_pieces(1)
     give_sources(1)

time: 43.5 us -> 43.6 us (level)
  no operation moved by 1% of the time
where the time goes in v7:
time: 43.6 us; the launch traced here: 43.5 us
  Pallas kernels  42.7 us (98%)
  local copies, waits for them, and re-layouts  0.75 us (2%)
    pallas_call x1, Pallas kernels, body(): pl.pallas_call(functools.partial(correlate_kernel, sizes), out_shape=jax....  42.7 us

profile of v7, /device:TPU:1, one launch (start us, length us, event | category | flops | bytes accessed | tf_op | source)
XLA Modules:
  0.0 43.5 jit_solution(15982756975395905528)
XLA Ops:
  0.0 42.7 %shard_map.17 = f32[8,8,512]{2,1,0:T(8,128)S(1)} custom-call(f32[256,512]{1,0:T(8,128)} %x_hbm.1), custom_call_target="tpu_custom_call" | custom-call | tf_op jit(solution)/shard_map/pallas_call | solution.py:325
  42.8 0.7 %copy.2 = f32[8,8,408]{2,1,0:T(8,128)} copy(f32[8,8,408]{2,0,1:T(8,128)S(1)} %slice_bitcast_fusion) | data formatting | bytes 208896 | tf_op jit(solution)/shard_map/transpose | solution.py:354
  (1 shorter events, 0.0 us)
